TPU v7x, 32 devices: a whole 2x2x4 slice. The times are simulated.
32 devices in a mesh: dp: 8 (over z, y), shard: 4 (over x, core).
Axes of the slice: x: 2, y: 2, z: 4, core: 2. Of those that a mesh axis runs over, the one named last changes fastest.
Arguments:
- tokens: bfloat16 [13312, 4096], P(('dp', 'shard')), may hold values from -6 to 6
- cotangent: bfloat16 [13312, 4096], P(('dp', 'shard')), may hold values from -6 to 6
- gate_up: bfloat16 [4, 4096, 256], P('shard'), may hold values from -0.09375 to 0.09375
- down: bfloat16 [4, 128, 4096], P('shard'), may hold values from -0.09375 to 0.09375
- kept_slots: int32 [2], replicated, may hold values from 0 to 3, as said below
Outputs:
- token_grad: bfloat16 [13312, 4096], P(('dp', 'shard'))
- grad_gate_up: bfloat16 [4, 4096, 256], P('shard', 'dp')
- grad_down: bfloat16 [4, 128, 4096], P('shard', None, 'dp')
Inputs may be any that keep to these rules, and one draw needn't show every extreme that they name: `kept_slots`: 2 distinct positions; position p is stored on index p // 1 of shard.
All inputs are finite; a program needn't handle non-finite values.
Results may differ from a plain program's by a relative error of at most 0.015.
Values may be sent and summed in bfloat16 or wider, within the bound.
A program may use at most 128 MiB of HBM per device.

v0:
```python
import math

import jax
import jax.numpy as jnp
from jax import lax
from jax.sharding import PartitionSpec as P


def spread(block, axis, source):
    block = jnp.where(lax.axis_index(axis) == source, block, jnp.zeros_like(block))
    return lax.psum(block, axis)


def body(tokens, cotangent, gate_up, down, kept_slots):
    slot_count = gate_up.shape[0]
    block_cols = down.shape[1]
    kept_count = kept_slots.shape[0]
    total_tokens = tokens.shape[0] * lax.axis_size("dp") * lax.axis_size("shard")
    scale_factor = 1.0 / math.sqrt(total_tokens)
    dx_total = jnp.zeros(tokens.shape, jnp.float32)
    pair_terms = []
    back_terms = []
    for kept_pos in range(kept_count):
        slot_id = kept_slots[kept_pos]
        local_slot = slot_id % slot_count
        owner_id = slot_id // slot_count
        own_pair = lax.dynamic_index_in_dim(gate_up, local_slot, 0, keepdims=False)
        own_back = lax.dynamic_index_in_dim(down, local_slot, 0, keepdims=False)
        w_pair, w_back = (spread(own_pair, "shard", owner_id), spread(own_back, "shard", owner_id))
        projected = jnp.dot(tokens, w_pair, preferred_element_type=jnp.float32)
        gate_pre = projected[:, :block_cols]
        up_pre = projected[:, block_cols:]
        sigmoid_gate = jax.nn.sigmoid(gate_pre)
        silu_gate = gate_pre * sigmoid_gate
        activated = (silu_gate * up_pre).astype(jnp.bfloat16)
        d_act = lax.dot_general(
            cotangent, w_back, (((1,), (1,)), ((), ())), preferred_element_type=jnp.float32
        )
        d_gate = d_act * up_pre * sigmoid_gate * (1.0 + gate_pre * (1.0 - sigmoid_gate))
        d_up = d_act * silu_gate
        d_projected = jnp.concatenate([d_gate, d_up], axis=1).astype(jnp.bfloat16)
        dx_total = dx_total + lax.dot_general(
            d_projected, w_pair, (((1,), (1,)), ((), ())), preferred_element_type=jnp.float32
        )
        pair_terms.append(
            lax.dot_general(
                tokens, d_projected, (((0,), (0,)), ((), ())), preferred_element_type=jnp.float32
            )
        )
        back_terms.append(
            lax.dot_general(
                activated, cotangent, (((0,), (0,)), ((), ())), preferred_element_type=jnp.float32
            )
        )
    pair_stack = jnp.stack(pair_terms)
    back_stack = jnp.stack(back_terms)
    pair_part, back_part = (
        lax.psum_scatter(
            pair_stack.astype(jnp.bfloat16), "dp", scatter_dimension=1, tiled=True
        ).astype(jnp.float32),
        lax.psum_scatter(
            back_stack.astype(jnp.bfloat16), "dp", scatter_dimension=2, tiled=True
        ).astype(jnp.float32),
    )
    pair_whole, back_whole = (
        lax.psum(pair_part.astype(jnp.bfloat16), "shard").astype(jnp.float32),
        lax.psum(back_part.astype(jnp.bfloat16), "shard").astype(jnp.float32),
    )
    my_slots = lax.axis_index("shard") * slot_count + jnp.arange(slot_count, dtype=jnp.int32)
    picking = (my_slots[:, None] == kept_slots[None, :]).astype(jnp.float32)
    pair_owned = jnp.einsum("sk,kab->sab", picking, pair_whole, precision=lax.Precision.HIGHEST)
    back_owned = jnp.einsum("sk,kab->sab", picking, back_whole, precision=lax.Precision.HIGHEST)
    return (
        dx_total.astype(jnp.bfloat16),
        (pair_owned * scale_factor).astype(jnp.bfloat16),
        (back_owned * scale_factor).astype(jnp.bfloat16),
    )


def solution(mesh):
    in_specs = (
        P(("dp", "shard"), None),
        P(("dp", "shard"), None),
        P("shard", None, None),
        P("shard", None, None),
        P(),
    )
    out_specs = (P(("dp", "shard"), None), P("shard", "dp", None), P("shard", None, "dp"))
    return jax.shard_map(body, mesh=mesh, in_specs=in_specs, out_specs=out_specs, check_vma=False)
```

profile of v0, /device:TPU:0, one launch (start us, length us, event | category | flops | bytes accessed | tf_op | source)
XLA Modules:
  0.0 355.7 jit_solution(2671473297520610019)
XLA Ops:
  7.2 1.4 fusion.21
  10.0 2.9 select_bitcast_fusion.2
  12.8 2.3 select_bitcast_fusion
  15.2 122.9 %all-reduce.7.cloned.1.call-done = (bf16[4096,256]{1,0:T(8,128)(2,1)}, bf16[128,4096]{1,0:T(8,128)(2,1)}, bf16[4096,256]{1,0:T(8,128)(2,1)}, bf16[128,4096]{1,0:T(8,128)(2,1)}) async-done(((bf16[4096,256]{1,0:T(8,128)(2,1)}, bf16[128,4096]{1,0:T(8,128)(2,1)}, bf16[4096,256]{1,0:T(8,128)(2,1)}, bf16[128,4096]{1,0:T(8,128)(2,1)}), (bf16[4096,256]{1,0:T(8,128)(2,1)}, bf16[128,4096]{1,0:T(8,128)(2,1)}, ...) | async-done | bytes 6291472 | tf_op jit(solution)/shard_map/psum | solution.py:11
  138.1 2.8 convolution_bitcast_fusion.1
  141.0 1.1 convolution_bitcast_fusion
  142.0 1.0 copy-done.1
  143.1 0.8 fusion.3
  143.9 0.8 fusion.2
  144.6 1.5 pad_maximum_fusion.1
  146.2 3.4 multiply_convert_fusion.3
  149.7 1.3 fusion.1
  152.0 1.1 multiply_convert_fusion.5
  153.8 1.3 fusion
  155.1 2.4 pad_maximum_fusion
  158.2 5.7 %fusion.11 = f32[416,4096]{1,0:T(8,128)} fusion(bf16[4096,256]{1,0:T(8,128)(2,1)} %get-tuple-element.5, bf16[416,128]{1,0:T(8,128)(2,1)} %copy-done.7, bf16[416,128]{1,0:T(8,128)(2,1)} %copy-done.6), kind=kOutput, calls=%fused_computation.38 | convolution fusion | flops 872841216 | bytes 9125888 | tf_op jit(solution)/shard_map/dot_general | solution.py:42
  163.8 50.8 %reduce-scatter.5.cloned.1.call-done = bf16[2,128,512]{2,1,0:T(8,128)(2,1)} async-done(((bf16[2,128,4096]{2,1,0:T(8,128)(2,1)}), bf16[2,128,512]{2,1,0:T(8,128)(2,1)}) %reduce-scatter.5.cloned.1.call-update) | async-done | bytes 262160 | tf_op jit(solution)/shard_map/reduce_scatter | solution.py:61
  214.7 91.0 %reduce-scatter.3.cloned.1.call-done = bf16[2,512,256]{1,2,0:T(8,128)(2,1)} async-done(((bf16[2,4096,256]{1,2,0:T(8,128)(2,1)}), bf16[2,512,256]{1,2,0:T(8,128)(2,1)}) %reduce-scatter.3.cloned.1.call-update) | async-done | bytes 524304 | tf_op jit(solution)/shard_map/reduce_scatter | solution.py:58
  305.7 6.4 %add_convert_fusion = bf16[416,4096]{1,0:T(8,128)(2,1)} fusion(f32[416,4096]{1,0:T(8,128)} %fusion.11, bf16[4096,256]{1,0:T(8,128)(2,1)} %get-tuple-element.7, bf16[416,128]{1,0:T(8,128)(2,1)} %copy-done.5, bf16[416,128]{1,0:T(8,128)(2,1)S(1)} %get-tuple-element.13), kind=kOutput, calls=%fused_computation | convolution fusion | flops 876249088 | bytes 12533760 | tf_op jit(solution)/shard_map/dot_general | solution.py:42
  312.1 30.5 %all-reduce.5.cloned.1.call-done = (bf16[2,512,256]{1,2,0:T(8,128)(2,1)}, bf16[2,128,512]{2,1,0:T(8,128)(2,1)}) async-done(((bf16[2,512,256]{1,2,0:T(8,128)(2,1)}, bf16[2,128,512]{2,1,0:T(8,128)(2,1)}), (bf16[2,512,256]{1,2,0:T(8,128)(2,1)}, bf16[2,128,512]{2,1,0:T(8,128)(2,1)})) %all-reduce.5.cloned.1.call-update) | async-done | bytes 786448 | tf_op jit(solution)/shard_map/psum | solution.py:66
  342.6 2.0 copy.8
  344.6 1.7 fusion.22
  346.3 0.8 fusion.5
  347.1 1.4 fusion.7
  (35 shorter events, 3.3 us)
Async XLA Ops:
  7.2 131.0 %copy-start = (bf16[416,4096]{1,0:T(8,128)(2,1)S(1)}, bf16[416,4096]{1,0:T(8,128)(2,1)}, u32[]{:S(2)}) copy-start(bf16[416,4096]{1,0:T(8,128)(2,1)} %param.5) | copy-start | bytes 10223620
  7.2 130.9 %all-reduce.7.cloned.1.call-start = ((), (), s32[]{:S(2)}) async-start(), calls=%async_computation.5 | async-start | bytes 12582912 | tf_op jit(solution)/shard_map/psum | solution.py:11
  9.9 2.9 copy-start.4
  15.1 199.5 %reduce-scatter.5.cloned.1.call-start = ((), (), s32[]{:S(2)}) async-start(), calls=%async_computation.3 | async-start | bytes 2359296 | tf_op jit(solution)/shard_map/reduce_scatter | solution.py:61
  138.1 2.8 copy-start.3
  140.9 2.9 copy-start.8
  140.9 2.1 copy-start.1
  143.1 1.6 copy-start.10
  146.2 159.5 %reduce-scatter.3.cloned.1.call-start = ((), (), s32[]{:S(2)}) async-start(), calls=%async_computation.2 | async-start | bytes 4718592 | tf_op jit(solution)/shard_map/reduce_scatter | solution.py:58
  149.6 1.3 copy-start.5
  149.6 2.0 copy-start.2
  149.6 2.1 copy-start.9
  149.7 2.4 copy-start.12
  153.1 0.6 copy-start.6
  153.1 0.7 copy-start.7
  157.5 0.7 copy-start.11
  157.5 185.1 %all-reduce.5.cloned.1.call-start = ((), (), s32[]{:S(2)}) async-start(), calls=%async_computation.4 | async-start | bytes 1572864 | tf_op jit(solution)/shard_map/psum | solution.py:66
Sparse Core Ops, SparseCore 0:
  15.2 122.8 all-reduce.6
  146.3 68.3 reduce-scatter.4
  218.3 87.3 reduce-scatter.2
  308.1 34.3 all-reduce.4
where the time goes:
time: 356 us
  waiting for transfers between devices  295 us (83%)
  matrix products  27.6 us (8%)
  between operations  15.2 us (4%)
  other arithmetic  10.5 us (3%)
  local copies, waits for them, and re-layouts  6.64 us (2%)
    psum x1, waiting for transfers between devices, spread(): return lax.psum(block, axis)  123 us
    reduce_scatter x1, waiting for transfers between devices, body(): lax.psum_scatter(pair_stack.astype(jnp.bfloat16), 'dp', scatter_dimension...  91 us
    reduce_scatter x1, waiting for transfers between devices, body(): lax.psum_scatter(back_stack.astype(jnp.bfloat16), 'dp', scatter_dimension...  50.8 us
    psum x1, waiting for transfers between devices, body(): lax.psum(pair_part.astype(jnp.bfloat16), 'shard').astype(jnp.float32)  30.5 us
    dot_general x2, matrix products, body(): lax.dot_general(d_projected, w_pair, (((1,), (1,)), ((), ())), preferred_...  12.1 us
  transfers between devices with their start and end apart: 4, of which 4 were waited for; matrix products, arithmetic and copies ran while one was open for 6% of the time, Pallas kernels for 0%

commit v1 on v0

v1 whole, which is shorter than its diff:
```python
import functools
import math

import jax
import jax.numpy as jnp
from jax import lax
from jax.experimental import pallas as pl
from jax.experimental.pallas import tpu as pltpu
from jax.sharding import PartitionSpec as P

MESH = pl.DeviceIdType.MESH
F32 = jnp.float32
BF16 = jnp.bfloat16
ALL = slice(None)


def fused(
    Z, Y, X, scale,
    kept, packed, tokens_hbm, cot_hbm,
    dx_hbm, gate_up_out, down_out,
    tok, cot, dxb, recv, sel, W, G, dproj, act, acc,
    r1, r2e, r2o, r3e, r3o, r4, fin,
    load_sem, own_sem, dx_sem, a2a_s, a2a_r, ag_s, ag_r, rs_s, rs_r, bc_s, bc_r,
):
    S = X * 2
    KB3 = W.shape[0]
    KB = KB3 // 3
    R = W.shape[-2]
    BLK = W.shape[-1]
    tile = Y * X * 2 * R
    d = lax.axis_index("dp")
    s = lax.axis_index("shard")
    me = {"z": d // Y, "y": d % Y, "x": s // 2, "c": s % 2}
    size = {"z": Z, "y": Y, "x": X, "c": 2}
    base = {"z": 0, "y": Z - 1, "x": Z - 1 + Y - 1, "c": Z - 1 + Y - 1 + X - 1}

    def device(co):
        return (co["z"] * Y + co["y"], co["x"] * 2 + co["c"])

    def peer(dim, o):
        co = dict(me)
        co[dim] = lax.rem(me[dim] + o, size[dim])
        return co

    def shard_peer(o):
        return lax.rem(s + o, S)

    load_tok = pltpu.make_async_copy(tokens_hbm, tok, load_sem.at[0])
    load_cot = pltpu.make_async_copy(cot_hbm, cot, load_sem.at[1])
    own = pltpu.make_async_copy(packed.at[:, d, s], recv.at[s], own_sem.at[0])
    own.start()

    barrier = pltpu.get_barrier_semaphore()
    greeted = [(d, shard_peer(o)) for o in range(1, S)]
    for dim in ("z", "y"):
        greeted += [device(peer(dim, o)) for o in range(1, size[dim])]
    for who in greeted:
        pl.semaphore_signal(barrier, inc=1, device_id=who, device_id_type=MESH)
    pl.semaphore_wait(barrier, len(greeted))

    a2a = []
    for o in range(1, S):
        to = shard_peer(o)
        a2a.append(pltpu.make_async_remote_copy(
            src_ref=packed.at[:, d, to], dst_ref=recv.at[s],
            send_sem=a2a_s.at[o - 1], recv_sem=a2a_r.at[o - 1],
            device_id=(d, to), device_id_type=MESH))
    for copy in a2a:
        copy.start()
    load_tok.start()
    load_cot.start()
    own.wait()
    for copy in a2a:
        copy.wait_recv()
    for k in range(KB):
        W[3 * k:3 * k + 3, me["z"], me["y"], me["x"], me["c"]] = recv[kept[k]]

    def gather_order(ch):
        return ("z", "y", "x", "c") if ch % 2 == 0 else ("z", "x", "y", "c")

    def gather_copies(ch, i):
        order = gather_order(ch)
        region = W.at[(ch,) + tuple(
            ALL if t in order[:i] else me[t] for t in ("z", "y", "x", "c"))]
        dim = order[i]
        return [pltpu.make_async_remote_copy(
            src_ref=region, dst_ref=region,
            send_sem=ag_s.at[ch, base[dim] + o - 1], recv_sem=ag_r.at[ch, base[dim] + o - 1],
            device_id=device(peer(dim, o)), device_id_type=MESH)
            for o in range(1, size[dim])]

    def gather_start(ch, i):
        for copy in gather_copies(ch, i):
            copy.start()

    def gather_wait(ch, i):
        for copy in gather_copies(ch, i):
            copy.wait_recv()

    for ch in range(KB3):
        gather_start(ch, 0)
    for i in range(3):
        for ch in range(KB3):
            gather_wait(ch, i)
            gather_start(ch, i + 1)

    def cols(z):
        return pl.ds(pl.multiple_of(z * tile, 128), tile)

    def w_tile(ch, z):
        return W[ch, z].reshape(tile, BLK)

    def pair_tile(k, z):
        return jnp.concatenate([w_tile(3 * k, z), w_tile(3 * k + 1, z)], axis=1)

    def forward(k):
        acc[...] = jnp.zeros_like(acc)

        @pl.loop(0, Z)
        def _(z):
            acc[:, :2 * BLK] += jnp.dot(tok[:, cols(z)], pair_tile(k, z), preferred_element_type=F32)
            acc[:, 2 * BLK:] += jnp.dot(cot[:, cols(z)], w_tile(3 * k + 2, z), preferred_element_type=F32)

        gate = acc[:, :BLK]
        up = acc[:, BLK:2 * BLK]
        d_act = acc[:, 2 * BLK:]
        sig = jax.nn.sigmoid(gate)
        silu = gate * sig
        act[k] = (silu * up).astype(BF16)
        dproj[k, :, :BLK] = (d_act * up * sig * (1.0 + gate * (1.0 - sig))).astype(BF16)
        dproj[k, :, BLK:] = (d_act * silu).astype(BF16)

    def grads(k):
        @pl.loop(0, Z)
        def _(z):
            pair = lax.dot_general(tok[:, cols(z)], dproj[k], (((0,), (0,)), ((), ())),
                                   preferred_element_type=F32).astype(BF16)
            G[3 * k, z] = pair[:, :BLK].reshape(Y, X, 2, R, BLK)
            G[3 * k + 1, z] = pair[:, BLK:].reshape(Y, X, 2, R, BLK)
            back = lax.dot_general(cot[:, cols(z)], act[k], (((0,), (0,)), ((), ())),
                                   preferred_element_type=F32).astype(BF16)
            G[3 * k + 2, z] = back.reshape(Y, X, 2, R, BLK)

    def dx_tile(z):
        total = jnp.zeros((tok.shape[0], tile), F32)
        for k in range(KB):
            total += lax.dot_general(dproj[k], pair_tile(k, z), (((1,), (1,)), ((), ())),
                                     preferred_element_type=F32)
        dxb[:, z * tile:(z + 1) * tile] = total.astype(BF16)
        dx_copy(z).start()

    def dx_copy(z):
        part = pl.ds(z * tile, tile)
        return pltpu.make_async_copy(dxb.at[:, part], dx_hbm.at[:, part], dx_sem.at[z])

    def scatter_order(ch):
        return ("c", "x", "y", "z") if ch % 2 == 0 else ("c", "y", "x", "z")

    def scatter_copies(ch, i):
        dim = scatter_order(ch)[i]
        h = ch // 2
        r2, r3 = (r2e, r3e) if ch % 2 == 0 else (r2o, r3o)
        out = []
        for o in range(1, size[dim]):
            to = peer(dim, o)
            at = to[dim]
            if i == 0:
                src, dst = G.at[ch, :, :, :, at], r1.at[ch]
            elif i == 1:
                src = r1.at[ch, :, :, at] if dim == "x" else r1.at[ch, :, at]
                dst = r2.at[h, o - 1]
            elif i == 2:
                src, dst = r2.at[h, 0, :, at], r3.at[h, o - 1]
            else:
                src, dst = r3.at[h, 0, at], r4.at[ch, o - 1]
            out.append(pltpu.make_async_remote_copy(
                src_ref=src, dst_ref=dst,
                send_sem=rs_s.at[ch, base[dim] + o - 1], recv_sem=rs_r.at[ch, base[dim] + o - 1],
                device_id=device(to), device_id_type=MESH))
        return out

    def scatter_start(ch, i):
        for copy in scatter_copies(ch, i):
            copy.start()

    def scatter_add(ch, i):
        for copy in scatter_copies(ch, i):
            copy.wait_recv()
        h = ch // 2
        r2, r3 = (r2e, r3e) if ch % 2 == 0 else (r2o, r3o)
        dim = scatter_order(ch)[i]
        at = me[dim]
        if i == 3:
            total = r3[h, 0, at].astype(F32)
            for o in range(1, Z):
                total += r4[ch, o - 1].astype(F32)
            fin[s, ch] = (total * scale).astype(BF16)
            return

        @pl.loop(0, Z)
        def _(z):
            if i == 0:
                r1[ch, z] = (G[ch, z, :, :, at].astype(F32) + r1[ch, z].astype(F32)).astype(BF16)
            elif i == 1:
                mine = r1[ch, z, :, at] if dim == "x" else r1[ch, z, at]
                total = mine.astype(F32)
                for o in range(1, size[dim]):
                    total += r2[h, o - 1, z].astype(F32)
                r2[h, 0, z] = total.astype(BF16)
            else:
                total = r2[h, 0, z, at].astype(F32)
                for o in range(1, size[dim]):
                    total += r3[h, o - 1, z].astype(F32)
                r3[h, 0, z] = total.astype(BF16)

    def last_copies(k):
        return [pltpu.make_async_remote_copy(
            src_ref=fin.at[s, pl.ds(3 * k, 3)], dst_ref=fin.at[s, pl.ds(3 * k, 3)],
            send_sem=bc_s.at[k, o - 1], recv_sem=bc_r.at[k, o - 1],
            device_id=(d, shard_peer(o)), device_id_type=MESH) for o in range(1, S)]

    load_tok.wait()
    load_cot.wait()
    for k in range(KB):
        for ch in range(3 * k, 3 * k + 3):
            gather_wait(ch, 3)
        forward(k)
        grads(k)
        for ch in range(3 * k, 3 * k + 3):
            scatter_start(ch, 0)
        if k > 0:
            for ch in range(3 * k - 3, 3 * k):
                scatter_add(ch, 0)
                scatter_start(ch, 1)
    for ch in range(KB3 - 3, KB3):
        scatter_add(ch, 0)
        scatter_start(ch, 1)
    half = Z // 2
    for z in range(half):
        dx_tile(z)
    for ch in range(KB3):
        scatter_add(ch, 1)
        scatter_start(ch, 2)
    for z in range(half, Z):
        dx_tile(z)
    for ch in range(KB3):
        scatter_add(ch, 2)
        scatter_start(ch, 3)
    for k in range(KB):
        for ch in range(3 * k, 3 * k + 3):
            scatter_add(ch, 3)
        for copy in last_copies(k):
            copy.start()
    for k in range(KB):
        for copy in last_copies(k):
            copy.wait_recv()

    for j in range(3):
        total = jnp.zeros((S * R, BLK), F32)
        for k in range(KB):
            hit = (kept[k] == s).astype(F32)
            total += hit * fin[:, 3 * k + j].reshape(S * R, BLK).astype(F32)
        if j < 2:
            gate_up_out[0, :, j * BLK:(j + 1) * BLK] = total.astype(BF16)
        else:
            down_out[0] = total.T.astype(BF16)

    for copy in a2a:
        copy.wait_send()
    for ch in range(KB3):
        for i in range(4):
            for copy in gather_copies(ch, i) + scatter_copies(ch, i):
                copy.wait_send()
    for k in range(KB):
        for copy in last_copies(k):
            copy.wait_send()
    for z in range(Z):
        dx_copy(z).wait()


def body(dp, shard, tokens, cotangent, gate_up, down, kept_slots):
    T, D = tokens.shape
    BLK = down.shape[1]
    KB = kept_slots.shape[0]
    Z = 4
    Y = dp // Z
    X = shard // 2
    S = shard
    R = D // (dp * shard)
    scale = 1.0 / math.sqrt(T * dp * shard)
    packed = jnp.stack([gate_up[0, :, :BLK], gate_up[0, :, BLK:], down[0].T])
    packed = packed.reshape(3, dp, shard, R, BLK)
    C = 3 * KB
    H = (C + 1) // 2
    L = (Z - 1) + (Y - 1) + (X - 1) + 1
    rows = D // dp
    vmem = pl.BlockSpec(memory_space=pltpu.VMEM)
    anym = pl.BlockSpec(memory_space=pl.ANY)
    V = pltpu.VMEM
    dma = pltpu.SemaphoreType.DMA
    return pl.pallas_call(
        functools.partial(fused, Z, Y, X, scale),
        out_shape=(
            jax.ShapeDtypeStruct((T, D), BF16),
            jax.ShapeDtypeStruct((1, rows, 2 * BLK), BF16),
            jax.ShapeDtypeStruct((1, BLK, rows), BF16),
        ),
        in_specs=[pl.BlockSpec(memory_space=pltpu.SMEM), anym, anym, anym],
        out_specs=(anym, vmem, vmem),
        scratch_shapes=[
            V((T, D), BF16), V((T, D), BF16), V((T, D), BF16),
            V((S, 3, R, BLK), BF16), V((8, 128), BF16),
            V((C, Z, Y, X, 2, R, BLK), BF16), V((C, Z, Y, X, 2, R, BLK), BF16),
            V((KB, T, 2 * BLK), BF16), V((KB, T, BLK), BF16), V((T, 3 * BLK), F32),
            V((C, Z, Y, X, R, BLK), BF16),
            V((H, X - 1, Z, Y, R, BLK), BF16), V((H, Y - 1, Z, X, R, BLK), BF16),
            V((H, Y - 1, Z, R, BLK), BF16), V((H, X - 1, Z, R, BLK), BF16),
            V((C, Z - 1, R, BLK), BF16), V((S, C, R, BLK), BF16),
            dma((2,)), dma((1,)), dma((Z,)), dma((S - 1,)), dma((S - 1,)),
            dma((C, L)), dma((C, L)), dma((C, L)), dma((C, L)),
            dma((KB, S - 1)), dma((KB, S - 1)),
        ],
        compiler_params=pltpu.CompilerParams(
            collective_id=0, has_side_effects=True, vmem_limit_bytes=58 * 1024 * 1024),
        name="fused_backward",
    )(kept_slots, packed, tokens, cotangent)


def solution(mesh):
    in_specs = (
        P(("dp", "shard"), None),
        P(("dp", "shard"), None),
        P("shard", None, None),
        P("shard", None, None),
        P(),
    )
    out_specs = (P(("dp", "shard"), None), P("shard", "dp", None), P("shard", None, "dp"))
    fn = functools.partial(body, mesh.shape["dp"], mesh.shape["shard"])
    return jax.shard_map(fn, mesh=mesh, in_specs=in_specs, out_specs=out_specs, check_vma=False)
```

time: 356 us -> 120 us (0.34)
  waiting for transfers between devices: 295 us -> 0 us
  Pallas kernels: 0 us -> 109 us
  matrix products: 27.6 us -> 0 us
  between operations: 15.2 us -> 0.68 us
  other arithmetic: 10.5 us -> 2 us
    psum x2 -> x0, waiting for transfers between devices: 153 us -> none  [the longest x1 123 us: spread(): return lax.psum(block, axis)]
    reduce_scatter x2 -> x0, waiting for transfers between devices: 142 us -> none  [the longest x1 91 us: body(): lax.psum_scatter(pair_stack.astype(jnp.bfloat16), 'dp', scatter_dimension...]
    pallas_call x0 -> x1, Pallas kernels: none -> 109 us  [body(): pl.pallas_call(functools.partial(fused, Z, Y, X, scale), out_shape=(jax.S...]
    dot_general x12 -> x0, matrix products: 27.6 us -> none  [the longest x2 12.1 us: body(): lax.dot_general(d_projected, w_pair, (((1,), (1,)), ((), ())), preferred_...]
    select_n x2 -> x0, other arithmetic: 5.15 us -> none  [spread(): jnp.where(lax.axis_index(axis) == source, block, jnp.zeros_like(block))]
  transfers between devices with their start and end apart: 4 -> 0, of which waited for: 4 -> 0; matrix products, arithmetic and copies ran while one was open for 6% -> 0% of each run, Pallas kernels for 0% -> 0%
where the time goes in v1:
time: 120 us
  Pallas kernels  109 us (91%)
  local copies, waits for them, and re-layouts  7.55 us (6%)
  other arithmetic  2 us (2%)
    pallas_call x1, Pallas kernels, body(): pl.pallas_call(functools.partial(fused, Z, Y, X, scale), out_shape=(jax.S...  109 us
    unnamed x9, local copies, waits for them, and re-layouts  5.65 us

profile of v1, /device:TPU:0, one launch (start us, length us, event | category | flops | bytes accessed | tf_op | source)
XLA Modules:
  0.0 119.7 jit_solution(2298704786724580565)
XLA Ops:
  0.6 0.0 copy-start
  0.6 1.8 %copy.8 = bf16[4096,128]{1,0:T(8,128)(2,1)S(1)} copy(bf16[4096,128]{0,1:T(8,128)(2,1)} %bitcast.9) | data formatting | bytes 2097152 | tf_op jit(solution)/shard_map/transpose | solution.py:291
  2.4 0.1 copy-done
  2.5 0.1 fusion
  2.7 2.0 %pad_maximum_fusion.packed = bf16[3,8,4,128,128]{4,3,2,1,0:T(8,128)(2,1)} fusion(bf16[1,8,4,128,128]{4,3,2,1,0:T(8,128)(2,1)S(1)} %bitcast.6, bf16[1,8,4,128,128]{4,3,2,1,0:T(8,128)(2,1)S(1)} %bitcast.8, bf16[1,8,4,128,128]{4,3,2,1,0:T(8,128)(2,1)S(1)} %bitcast.7), kind=kLoop, calls=%fused_computation | loop fusion | flops 3145728 | bytes 6291456 | tf_op jit(solution)/shard_map/stack | solution.py:291
  4.7 109.5 %fused_backward.1 = (bf16[416,4096]{1,0:T(8,128)(2,1)}, bf16[1,512,256]{2,1,0:T(8,128)(2,1)}, bf16[1,128,512]{2,1,0:T(8,128)(2,1)}) custom-call(s32[2]{0:T(128)} %kept.1, bf16[3,8,4,128,128]{4,3,2,1,0:T(8,128)(2,1)} %pad_maximum_fusion.packed, bf16[416,4096]{1,0:T(8,128)(2,1)} %tokens_hbm.1, bf16[416,4096]{1,0:T(8,128)(2,1)} %cot_hbm.1), custom_call_target="tpu_custom_call" | custom-call | tf_op jit(solution)/shard_map/fused_backward/pallas_call | solution.py:301
  114.1 0.0 copy-start.1
  114.2 0.0 copy-start.2
  114.2 4.2 %copy.12 = bf16[416,4096]{1,0:T(8,128)(2,1)} copy(bf16[416,4096]{1,0:T(8,128)(2,1)} %get-tuple-element.8) | data formatting | bytes 6815744
  118.3 0.0 copy-done.1
  118.3 0.7 copy.13
  119.0 0.0 copy-done.2
  119.0 0.7 copy.14
Async XLA Ops:
  0.6 1.9 %copy-start = (bf16[1,4096,256]{2,1,0:T(8,128)(2,1)S(1)}, bf16[1,4096,256]{2,1,0:T(8,128)(2,1)}, u32[]{:S(2)}) copy-start(bf16[1,4096,256]{2,1,0:T(8,128)(2,1)} %param.7) | copy-start | bytes 6291460
  114.1 4.2 %copy-start.1 = (bf16[1,512,256]{2,1,0:T(8,128)(2,1)S(1)}, bf16[1,512,256]{2,1,0:T(8,128)(2,1)}, u32[]{:S(2)}) copy-start(bf16[1,512,256]{2,1,0:T(8,128)(2,1)} %get-tuple-element.9) | copy-start | bytes 786436
  114.2 4.9 %copy-start.2 = (bf16[1,128,512]{2,1,0:T(8,128)(2,1)S(1)}, bf16[1,128,512]{2,1,0:T(8,128)(2,1)}, u32[]{:S(2)}) copy-start(bf16[1,128,512]{2,1,0:T(8,128)(2,1)} %get-tuple-element.10) | copy-start | bytes 393220

commit v2 on v1

v2 whole, which is shorter than its diff:
```python
import functools
import math

import jax
import jax.numpy as jnp
from jax import lax
from jax.experimental import pallas as pl
from jax.experimental.pallas import tpu as pltpu
from jax.sharding import PartitionSpec as P

MESH = pl.DeviceIdType.MESH
F32 = jnp.float32
BF16 = jnp.bfloat16
ALL = slice(None)


def fused(
    Z, Y, X, scale,
    kept, pair_hbm, back_hbm, tokens_hbm, cot_hbm,
    dx_hbm, gate_up_out, down_out,
    tok, cot, dxb, recv_pair, recv_back, W, G, dproj, act, acc,
    r1, r2e, r2o, r3e, r3o, rz, r4, fin,
    load_sem, own_sem, dx_sem, a2a_s, a2a_r, ag_s, ag_r, rs_s, rs_r, bc_s, bc_r,
):
    S = X * 2
    KB3 = W.shape[0]
    KB = KB3 // 3
    R = W.shape[-2]
    BLK = W.shape[-1]
    tile = Y * X * 2 * R
    d = lax.axis_index("dp")
    s = lax.axis_index("shard")
    me = {"z": d // Y, "y": d % Y, "x": s // 2, "c": s % 2}
    size = {"z": Z, "y": Y, "x": X, "c": 2}
    hz = Z // 2
    base = {("z", 0): 0, ("c", 0): Z - 1}
    base["y", 0] = Z
    base["y", 1] = base["y", 0] + Y - 1
    base["x", 0] = base["y", 1] + Y - 1
    base["x", 1] = base["x", 0] + X - 1
    flipped = len(back_hbm.shape) == 2

    def device(co):
        return (co["z"] * Y + co["y"], co["x"] * 2 + co["c"])

    def peer(dim, o):
        co = dict(me)
        co[dim] = lax.rem(me[dim] + o, size[dim])
        return co

    def shard_peer(o):
        return lax.rem(s + o, S)

    load_tok = pltpu.make_async_copy(tokens_hbm, tok, load_sem.at[0])
    load_cot = pltpu.make_async_copy(cot_hbm, cot, load_sem.at[1])

    def pieces(who):
        row = pl.multiple_of((d * S + who) * R, R)
        if flipped:
            return (pair_hbm.at[0, pl.ds(row, R)], back_hbm.at[:, pl.ds(row, R)])
        return (pair_hbm.at[0, pl.ds(row, R)], back_hbm.at[0, pl.ds(row, R)])

    landing = (recv_pair.at[s], recv_back.at[s])
    own = [pltpu.make_async_copy(pieces(s)[p], landing[p], own_sem.at[p]) for p in range(2)]
    for copy in own:
        copy.start()

    barrier = pltpu.get_barrier_semaphore()
    greeted = [(d, shard_peer(o)) for o in range(1, S)]
    for dim in ("z", "y"):
        greeted += [device(peer(dim, o)) for o in range(1, size[dim])]
    for who in greeted:
        pl.semaphore_signal(barrier, inc=1, device_id=who, device_id_type=MESH)
    pl.semaphore_wait(barrier, len(greeted))

    a2a = []
    for o in range(1, S):
        to = shard_peer(o)
        for p in range(2):
            a2a.append(pltpu.make_async_remote_copy(
                src_ref=pieces(to)[p], dst_ref=landing[p],
                send_sem=a2a_s.at[p, o - 1], recv_sem=a2a_r.at[p, o - 1],
                device_id=(d, to), device_id_type=MESH))
    for copy in a2a:
        copy.start()
    load_tok.start()
    load_cot.start()
    for copy in own:
        copy.wait()
    for copy in a2a:
        copy.wait_recv()
    for k in range(KB):
        at = (me["z"], me["y"], me["x"], me["c"])
        pair = recv_pair[kept[k]]
        back = recv_back[kept[k]]
        if flipped:
            back = back.astype(F32).T.astype(BF16)
        W[(3 * k,) + at] = pair[:, :BLK]
        W[(3 * k + 1,) + at] = pair[:, BLK:]
        W[(3 * k + 2,) + at] = back

    def gather_copies(ch, i):
        if i == 0:
            moves = [("z", 0, (me["z"], me["y"], me["x"], me["c"]))]
        elif i == 3:
            moves = [("c", 0, (ALL, ALL, ALL, me["c"]))]
        else:
            moves = []
            for h in range(2):
                first = "yx"[h]
                dim = first if i == 1 else "xy"[h]
                y = ALL if i == 2 and first == "y" else me["y"]
                x = ALL if i == 2 and first == "x" else me["x"]
                moves.append((dim, h, (pl.ds(h * hz, hz), y, x, me["c"])))
        out = []
        for dim, h, at in moves:
            region = W.at[(ch,) + at]
            for o in range(1, size[dim]):
                n = base[dim, h] + o - 1
                out.append(pltpu.make_async_remote_copy(
                    src_ref=region, dst_ref=region,
                    send_sem=ag_s.at[ch, n], recv_sem=ag_r.at[ch, n],
                    device_id=device(peer(dim, o)), device_id_type=MESH))
        return out

    def gather_start(ch, i):
        for copy in gather_copies(ch, i):
            copy.start()

    def gather_wait(ch, i):
        for copy in gather_copies(ch, i):
            copy.wait_recv()

    def cols(z):
        return pl.ds(pl.multiple_of(z * tile, 128), tile)

    def w_tile(ch, z):
        return W[ch, z].reshape(tile, BLK)

    def pair_tile(k, z):
        return jnp.concatenate([w_tile(3 * k, z), w_tile(3 * k + 1, z)], axis=1)

    def forward(k):
        acc[...] = jnp.zeros_like(acc)

        @pl.loop(0, Z)
        def _(z):
            acc[:, :2 * BLK] += jnp.dot(tok[:, cols(z)], pair_tile(k, z), preferred_element_type=F32)
            acc[:, 2 * BLK:] += jnp.dot(cot[:, cols(z)], w_tile(3 * k + 2, z), preferred_element_type=F32)

        gate = acc[:, :BLK]
        up = acc[:, BLK:2 * BLK]
        d_act = acc[:, 2 * BLK:]
        sig = jax.nn.sigmoid(gate)
        silu = gate * sig
        act[k] = (silu * up).astype(BF16)
        dproj[k, :, :BLK] = (d_act * up * sig * (1.0 + gate * (1.0 - sig))).astype(BF16)
        dproj[k, :, BLK:] = (d_act * silu).astype(BF16)

    def grads(k):
        @pl.loop(0, Z)
        def _(z):
            pair = lax.dot_general(tok[:, cols(z)], dproj[k], (((0,), (0,)), ((), ())),
                                   preferred_element_type=F32).astype(BF16)
            G[3 * k, z] = pair[:, :BLK].reshape(Y, X, 2, R, BLK)
            G[3 * k + 1, z] = pair[:, BLK:].reshape(Y, X, 2, R, BLK)
            back = lax.dot_general(cot[:, cols(z)], act[k], (((0,), (0,)), ((), ())),
                                   preferred_element_type=F32).astype(BF16)
            G[3 * k + 2, z] = back.reshape(Y, X, 2, R, BLK)

    def dx_tile(z):
        total = jnp.zeros((tok.shape[0], tile), F32)
        for k in range(KB):
            total += lax.dot_general(dproj[k], pair_tile(k, z), (((1,), (1,)), ((), ())),
                                     preferred_element_type=F32)
        dxb[:, z * tile:(z + 1) * tile] = total.astype(BF16)
        dx_copy(z).start()

    def dx_copy(z):
        part = pl.ds(z * tile, tile)
        return pltpu.make_async_copy(dxb.at[:, part], dx_hbm.at[:, part], dx_sem.at[z])

    def scatter_moves(i):
        if i == 0:
            return [("c", 0)]
        if i == 3:
            return [("z", 0)]
        return [("xy"[h] if i == 1 else "yx"[h], h) for h in range(2)]

    def scatter_copies(ch, i):
        out = []
        for dim, h in scatter_moves(i):
            r2, r3 = ((r2e, r3e), (r2o, r3o))[h]
            zs = pl.ds(h * hz, hz)
            for o in range(1, size[dim]):
                to = peer(dim, o)
                at = to[dim]
                if i == 0:
                    src, dst = G.at[ch, :, :, :, at], r1.at[ch]
                elif i == 1:
                    src = r1.at[ch, zs, :, at] if dim == "x" else r1.at[ch, zs, at]
                    dst = r2.at[ch, o - 1]
                elif i == 2:
                    src, dst = r2.at[ch, 0, :, at], r3.at[ch, o - 1]
                else:
                    src, dst = rz.at[ch, at], r4.at[ch, o - 1]
                n = base[dim, h] + o - 1
                out.append(pltpu.make_async_remote_copy(
                    src_ref=src, dst_ref=dst,
                    send_sem=rs_s.at[ch, n], recv_sem=rs_r.at[ch, n],
                    device_id=device(to), device_id_type=MESH))
        return out

    def scatter_start(ch, i):
        for copy in scatter_copies(ch, i):
            copy.start()

    def scatter_add(ch, i):
        for copy in scatter_copies(ch, i):
            copy.wait_recv()
        if i == 3:
            total = rz[ch, me["z"]].astype(F32)
            for o in range(1, Z):
                total += r4[ch, o - 1].astype(F32)
            fin[s, ch] = (total * scale).astype(BF16)
            return
        if i == 0:
            @pl.loop(0, Z)
            def _(z):
                r1[ch, z] = (G[ch, z, :, :, me["c"]].astype(F32) + r1[ch, z].astype(F32)).astype(BF16)
            return
        for dim, h in scatter_moves(i):
            r2, r3 = ((r2e, r3e), (r2o, r3o))[h]
            at = me[dim]
            for z in range(hz):
                if i == 1:
                    zz = h * hz + z
                    mine = r1[ch, zz, :, at] if dim == "x" else r1[ch, zz, at]
                    total = mine.astype(F32)
                    for o in range(1, size[dim]):
                        total += r2[ch, o - 1, z].astype(F32)
                    r2[ch, 0, z] = total.astype(BF16)
                else:
                    total = r2[ch, 0, z, at].astype(F32)
                    for o in range(1, size[dim]):
                        total += r3[ch, o - 1, z].astype(F32)
                    rz[ch, h * hz + z] = total.astype(BF16)

    def last_copies(k):
        return [pltpu.make_async_remote_copy(
            src_ref=fin.at[s, pl.ds(3 * k, 3)], dst_ref=fin.at[s, pl.ds(3 * k, 3)],
            send_sem=bc_s.at[k, o - 1], recv_sem=bc_r.at[k, o - 1],
            device_id=(d, shard_peer(o)), device_id_type=MESH) for o in range(1, S)]

    early = range(0, 3)
    late = range(3, KB3)
    gather_start(0, 0)
    for t in range(KB3 + 3):
        for ch in range(KB3 - 1, -1, -1):
            i = t - ch
            if 0 <= i < 3:
                gather_wait(ch, i)
                if i == 0 and ch + 1 < KB3:
                    gather_start(ch + 1, 0)
                gather_start(ch, i + 1)
        if t == 5:
            load_tok.wait()
            load_cot.wait()
            for ch in early:
                gather_wait(ch, 3)
            forward(0)
        if t == 6:
            grads(0)
            for ch in early:
                scatter_start(ch, 0)
        if t == 7:
            for ch in early:
                scatter_add(ch, 0)
                scatter_start(ch, 1)
    for ch in late:
        gather_wait(ch, 3)
    for k in range(1, KB):
        forward(k)
        grads(k)
    for ch in late:
        scatter_start(ch, 0)
    for ch in early:
        scatter_add(ch, 1)
        scatter_start(ch, 2)
    for ch in late:
        scatter_add(ch, 0)
        scatter_start(ch, 1)
    half = Z // 2
    for z in range(half):
        dx_tile(z)
    for ch in early:
        scatter_add(ch, 2)
        scatter_start(ch, 3)
    for z in range(half, Z):
        dx_tile(z)
    for ch in early:
        scatter_add(ch, 3)
    for copy in last_copies(0):
        copy.start()
    for i in range(1, 3):
        for ch in late:
            scatter_add(ch, i)
            scatter_start(ch, i + 1)
    for k in range(1, KB):
        for ch in range(3 * k, 3 * k + 3):
            scatter_add(ch, 3)
        for copy in last_copies(k):
            copy.start()
    for k in range(KB):
        for copy in last_copies(k):
            copy.wait_recv()

    for j in range(3):
        total = jnp.zeros((S * R, BLK), F32)
        for k in range(KB):
            hit = (kept[k] == s).astype(F32)
            total += hit * fin[:, 3 * k + j].reshape(S * R, BLK).astype(F32)
        if j < 2:
            gate_up_out[0, :, j * BLK:(j + 1) * BLK] = total.astype(BF16)
        else:
            down_out[0] = total.T.astype(BF16)

    for copy in a2a:
        copy.wait_send()
    for ch in range(KB3):
        for i in range(4):
            for copy in gather_copies(ch, i) + scatter_copies(ch, i):
                copy.wait_send()
    for k in range(KB):
        for copy in last_copies(k):
            copy.wait_send()
    for z in range(Z):
        dx_copy(z).wait()


def body(dp, shard, tokens, cotangent, gate_up, down, kept_slots):
    T, D = tokens.shape
    BLK = down.shape[1]
    KB = kept_slots.shape[0]
    Z = 4
    Y = dp // Z
    X = shard // 2
    S = shard
    R = D // (dp * shard)
    scale = 1.0 / math.sqrt(T * dp * shard)
    if R % 128 == 0:
        back, back_piece = down[0], (BLK, R)
    else:
        back, back_piece = down[0].T[None], (R, BLK)
    C = 3 * KB
    H = Z // 2
    L = Z + 2 * (Y - 1) + 2 * (X - 1)
    rows = D // dp
    vmem = pl.BlockSpec(memory_space=pltpu.VMEM)
    anym = pl.BlockSpec(memory_space=pl.ANY)
    V = pltpu.VMEM
    dma = pltpu.SemaphoreType.DMA
    return pl.pallas_call(
        functools.partial(fused, Z, Y, X, scale),
        out_shape=(
            jax.ShapeDtypeStruct((T, D), BF16),
            jax.ShapeDtypeStruct((1, rows, 2 * BLK), BF16),
            jax.ShapeDtypeStruct((1, BLK, rows), BF16),
        ),
        in_specs=[pl.BlockSpec(memory_space=pltpu.SMEM), anym, anym, anym, anym],
        out_specs=(anym, vmem, vmem),
        scratch_shapes=[
            V((T, D), BF16), V((T, D), BF16), V((T, D), BF16),
            V((S, R, 2 * BLK), BF16), V((S,) + back_piece, BF16),
            V((C, Z, Y, X, 2, R, BLK), BF16), V((C, Z, Y, X, 2, R, BLK), BF16),
            V((KB, T, 2 * BLK), BF16), V((KB, T, BLK), BF16), V((T, 3 * BLK), F32),
            V((C, Z, Y, X, R, BLK), BF16),
            V((C, X - 1, H, Y, R, BLK), BF16), V((C, Y - 1, H, X, R, BLK), BF16),
            V((C, Y - 1, H, R, BLK), BF16), V((C, X - 1, H, R, BLK), BF16),
            V((C, Z, R, BLK), BF16),
            V((C, Z - 1, R, BLK), BF16), V((S, C, R, BLK), BF16),
            dma((2,)), dma((2,)), dma((Z,)), dma((2, S - 1)), dma((2, S - 1)),
            dma((C, L)), dma((C, L)), dma((C, L)), dma((C, L)),
            dma((KB, S - 1)), dma((KB, S - 1)),
        ],
        compiler_params=pltpu.CompilerParams(
            collective_id=0, has_side_effects=True, vmem_limit_bytes=58 * 1024 * 1024),
        name="fused_backward",
    )(kept_slots, gate_up, back, tokens, cotangent)


def solution(mesh):
    in_specs = (
        P(("dp", "shard"), None),
        P(("dp", "shard"), None),
        P("shard", None, None),
        P("shard", None, None),
        P(),
    )
    out_specs = (P(("dp", "shard"), None), P("shard", "dp", None), P("shard", None, "dp"))
    fn = functools.partial(body, mesh.shape["dp"], mesh.shape["shard"])
    return jax.shard_map(fn, mesh=mesh, in_specs=in_specs, out_specs=out_specs, check_vma=False)
```

time: 120 us -> 102 us (0.85)
  Pallas kernels: 109 us -> 96.1 us
  local copies, waits for them, and re-layouts: 7.55 us -> 5.52 us
  other arithmetic: 2 us -> 0 us
    pallas_call x1, Pallas kernels: 109 us -> 96.1 us  [body(): pl.pallas_call(functools.partial(fused, Z, Y, X, scale), out_shape=(jax.S...]
    another operation x1 -> x0, other arithmetic: 2 us -> none  [body(): packed = jnp.stack([gate_up[0, :, :BLK], gate_up[0, :, BLK:], down[0].T])]
    transpose x1 -> x0, local copies, waits for them, and re-layouts: 1.76 us -> none  [body(): packed = jnp.stack([gate_up[0, :, :BLK], gate_up[0, :, BLK:], down[0].T])]
    unnamed x9 -> x7, local copies, waits for them, and re-layouts: 5.65 us -> 5.52 us
where the time goes in v2:
time: 102 us
  Pallas kernels  96.1 us (94%)
  local copies, waits for them, and re-layouts  5.52 us (5%)
    pallas_call x1, Pallas kernels, body(): pl.pallas_call(functools.partial(fused, Z, Y, X, scale), out_shape=(jax.S...  96.1 us
    unnamed x7, local copies, waits for them, and re-layouts  5.52 us

profile of v2, /device:TPU:0, one launch (start us, length us, event | category | flops | bytes accessed | tf_op | source)
XLA Modules:
  0.0 102.2 jit_solution(4686182116172057727)
XLA Ops:
  0.6 96.1 %fused_backward.1 = (bf16[416,4096]{1,0:T(8,128)(2,1)}, bf16[1,512,256]{2,1,0:T(8,128)(2,1)}, bf16[1,128,512]{2,1,0:T(8,128)(2,1)}) custom-call(s32[2]{0:T(128)} %kept.1, bf16[1,4096,256]{2,1,0:T(8,128)(2,1)} %pair_hbm.1, bf16[128,4096]{1,0:T(8,128)(2,1)} %bitcast.1, bf16[416,4096]{1,0:T(8,128)(2,1)} %tokens_hbm.1, bf16[416,4096]{1,0:T(8,128)(2,1)} %cot_hbm.1), custom_call_target="tpu_custom_call" | custom-call | tf_op jit(solution)/shard_map/fused_backward/pallas_call | solution.py:363
  96.7 0.0 copy-start
  96.7 0.0 copy-start.1
  96.7 4.2 %copy.11 = bf16[416,4096]{1,0:T(8,128)(2,1)} copy(bf16[416,4096]{1,0:T(8,128)(2,1)} %get-tuple-element.6) | data formatting | bytes 6815744
  100.9 0.0 copy-done
  100.9 0.7 copy.12
  101.6 0.0 copy-done.1
  101.6 0.7 copy.13
Async XLA Ops:
  96.7 4.2 %copy-start = (bf16[1,512,256]{2,1,0:T(8,128)(2,1)S(1)}, bf16[1,512,256]{2,1,0:T(8,128)(2,1)}, u32[]{:S(2)}) copy-start(bf16[1,512,256]{2,1,0:T(8,128)(2,1)} %get-tuple-element.7) | copy-start | bytes 786436
  96.7 4.9 %copy-start.1 = (bf16[1,128,512]{2,1,0:T(8,128)(2,1)S(1)}, bf16[1,128,512]{2,1,0:T(8,128)(2,1)}, u32[]{:S(2)}) copy-start(bf16[1,128,512]{2,1,0:T(8,128)(2,1)} %get-tuple-element.8) | copy-start | bytes 393220

commit v3 on v2

--- a/solution.py
+++ b/solution.py
@@ -358,6 +358,7 @@
     rows = D // dp
     vmem = pl.BlockSpec(memory_space=pltpu.VMEM)
     anym = pl.BlockSpec(memory_space=pl.ANY)
+    hbm = pl.BlockSpec(memory_space=pltpu.HBM)
     V = pltpu.VMEM
     dma = pltpu.SemaphoreType.DMA
     return pl.pallas_call(
@@ -367,7 +368,7 @@
             jax.ShapeDtypeStruct((1, rows, 2 * BLK), BF16),
             jax.ShapeDtypeStruct((1, BLK, rows), BF16),
         ),
-        in_specs=[pl.BlockSpec(memory_space=pltpu.SMEM), anym, anym, anym, anym],
+        in_specs=[pl.BlockSpec(memory_space=pltpu.SMEM), hbm, hbm, hbm, hbm],
         out_specs=(anym, vmem, vmem),
         scratch_shapes=[
             V((T, D), BF16), V((T, D), BF16), V((T, D), BF16),
@@ -384,9 +385,10 @@
             dma((KB, S - 1)), dma((KB, S - 1)),
         ],
         compiler_params=pltpu.CompilerParams(
-            collective_id=0, has_side_effects=True, vmem_limit_bytes=58 * 1024 * 1024),
+            collective_id=0, has_side_effects=True, vmem_limit_bytes=40 * 1024 * 1024),
         name="fused_backward",
-    )(kept_slots, gate_up, back, tokens, cotangent)
+    )(kept_slots, *(pltpu.with_memory_space_constraint(v, pltpu.HBM)
+                   for v in (gate_up, back, tokens, cotangent)))
 
 
 def solution(mesh):

time: 102 us -> 100 us (0.980)
  local copies, waits for them, and re-layouts: 5.52 us -> 3.76 us
    unnamed x7 -> x5, local copies, waits for them, and re-layouts: 5.52 us -> 3.76 us
where the time goes in v3:
time: 100 us
  Pallas kernels  95.6 us (96%)
  local copies, waits for them, and re-layouts  3.76 us (4%)
    pallas_call x1, Pallas kernels, body(): pl.pallas_call(functools.partial(fused, Z, Y, X, scale), out_shape=(jax.S...  95.6 us
    unnamed x5, local copies, waits for them, and re-layouts  3.76 us

profile of v3, /device:TPU:0, one launch (start us, length us, event | category | flops | bytes accessed | tf_op | source)
XLA Modules:
  0.0 100.0 jit_solution(10215309198345178396)
XLA Ops:
  0.6 0.0 copy-start
  0.6 0.6 copy-done
  1.3 95.6 %fused_backward.1 = (bf16[416,4096]{1,0:T(8,128)(2,1)S(1)}, bf16[1,512,256]{2,1,0:T(8,128)(2,1)S(1)}, bf16[1,128,512]{2,1,0:T(8,128)(2,1)S(1)}) custom-call(s32[2]{0:T(128)S(1)} %copy-done, bf16[1,4096,256]{2,1,0:T(8,128)(2,1)} %pair_hbm.1, bf16[128,4096]{1,0:T(8,128)(2,1)} %bitcast.1, bf16[416,4096]{1,0:T(8,128)(2,1)} %tokens_hbm.1, bf16[416,4096]{1,0:T(8,128)(2,1)} %cot_hbm.1), custom_call_target="tpu_custom_call" | custom-call | tf_op jit(solution)/shard_map/fused_backward/pallas_call | solution.py:364
  96.9 1.8 %copy.11 = bf16[416,4096]{1,0:T(8,128)(2,1)} copy(bf16[416,4096]{1,0:T(8,128)(2,1)S(1)} %get-tuple-element.6) | data formatting | bytes 6815744
  98.6 0.7 copy.12
  99.3 0.7 copy.13
Async XLA Ops:
  0.6 0.7 copy-start

commit v4 on v3

--- a/solution.py
+++ b/solution.py
@@ -164,9 +164,16 @@
                                    preferred_element_type=F32).astype(BF16)
             G[3 * k, z] = pair[:, :BLK].reshape(Y, X, 2, R, BLK)
             G[3 * k + 1, z] = pair[:, BLK:].reshape(Y, X, 2, R, BLK)
+        scatter_start(3 * k, 0)
+        scatter_start(3 * k + 1, 0)
+
+        @pl.loop(0, Z)
+        def _(z):
             back = lax.dot_general(cot[:, cols(z)], act[k], (((0,), (0,)), ((), ())),
                                    preferred_element_type=F32).astype(BF16)
             G[3 * k + 2, z] = back.reshape(Y, X, 2, R, BLK)
+
+        scatter_start(3 * k + 2, 0)
 
     def dx_tile(z):
         total = jnp.zeros((tok.shape[0], tile), F32)
@@ -255,13 +262,14 @@
     early = range(0, 3)
     late = range(3, KB3)
     gather_start(0, 0)
+    gather_start(1, 0)
     for t in range(KB3 + 3):
         for ch in range(KB3 - 1, -1, -1):
             i = t - ch
             if 0 <= i < 3:
                 gather_wait(ch, i)
-                if i == 0 and ch + 1 < KB3:
-                    gather_start(ch + 1, 0)
+                if i == 0 and ch + 2 < KB3:
+                    gather_start(ch + 2, 0)
                 gather_start(ch, i + 1)
         if t == 5:
             load_tok.wait()
@@ -271,8 +279,6 @@
             forward(0)
         if t == 6:
             grads(0)
-            for ch in early:
-                scatter_start(ch, 0)
         if t == 7:
             for ch in early:
                 scatter_add(ch, 0)
@@ -282,8 +288,6 @@
     for k in range(1, KB):
         forward(k)
         grads(k)
-    for ch in late:
-        scatter_start(ch, 0)
     for ch in early:
         scatter_add(ch, 1)
         scatter_start(ch, 2)

time: 100 us -> 97.2 us (0.972)
  Pallas kernels: 95.6 us -> 92.2 us
    pallas_call x1, Pallas kernels: 95.6 us -> 92.2 us  [body(): pl.pallas_call(functools.partial(fused, Z, Y, X, scale), out_shape=(jax.S...]
where the time goes in v4:
time: 97.2 us; the launch traced here: 96.6 us
  Pallas kernels  92.2 us (95%)
  local copies, waits for them, and re-layouts  3.76 us (4%)
    pallas_call x1, Pallas kernels, body(): pl.pallas_call(functools.partial(fused, Z, Y, X, scale), out_shape=(jax.S...  92.2 us
    unnamed x5, local copies, waits for them, and re-layouts  3.76 us

profile of v4, /device:TPU:0, one launch (start us, length us, event | category | flops | bytes accessed | tf_op | source)
XLA Modules:
  0.0 96.6 jit_solution(15746220057728329742)
XLA Ops:
  0.6 0.0 copy-start
  0.6 0.6 copy-done
  1.3 92.2 %fused_backward.1 = (bf16[416,4096]{1,0:T(8,128)(2,1)S(1)}, bf16[1,512,256]{2,1,0:T(8,128)(2,1)S(1)}, bf16[1,128,512]{2,1,0:T(8,128)(2,1)S(1)}) custom-call(s32[2]{0:T(128)S(1)} %copy-done, bf16[1,4096,256]{2,1,0:T(8,128)(2,1)} %pair_hbm.1, bf16[128,4096]{1,0:T(8,128)(2,1)} %bitcast.1, bf16[416,4096]{1,0:T(8,128)(2,1)} %tokens_hbm.1, bf16[416,4096]{1,0:T(8,128)(2,1)} %cot_hbm.1), custom_call_target="tpu_custom_call" | custom-call | tf_op jit(solution)/shard_map/fused_backward/pallas_call | solution.py:368
  93.5 1.8 %copy.11 = bf16[416,4096]{1,0:T(8,128)(2,1)} copy(bf16[416,4096]{1,0:T(8,128)(2,1)S(1)} %get-tuple-element.6) | data formatting | bytes 6815744
  95.3 0.7 copy.12
  96.0 0.7 copy.13
Async XLA Ops:
  0.6 0.7 copy-start
